TPU v7x, 512 devices: a whole 4x8x8 slice. The times are simulated.
512 devices in a mesh: row: 32 (over x, y), col: 16 (over z, core).
Axes of the slice: x: 4, y: 8, z: 8, core: 2. Of those that a mesh axis runs over, the one named last changes fastest.
Arguments:
- features: bfloat16 [131072, 128], P(('row', 'col')), may hold values from -6 to 6
- degree: int32 [131072], P(('row', 'col')), may hold values from 1 to 256
- weight: bfloat16 [128, 128], replicated, may hold values from -0.5 to 0.5
- bias: float32 [128], replicated, may hold values from -3 to 3
- cotangent: bfloat16 [131072, 128], P(('row', 'col')), may hold values from -8 to 8
- tile_rows: int32 [32, 16, 128], P('row', 'col'), may hold values from 0 to 31
- tile_cols: int32 [32, 16, 128], P('row', 'col'), may hold values from 0 to 63
- tile_count: int32 [32, 16, 1], P('row', 'col'), may hold values from 32 to 128, as said below
- tile_codes: int32 [32, 16, 128, 256], P('row', 'col'), may hold values from 0 to 4095
Outputs:
- hidden: bfloat16 [131072, 128], P(('row', 'col'))
- grad_features: bfloat16 [131072, 128], P(('row', 'col'))
- grad_weight: float32 [128, 128], replicated
- grad_bias: float32 [128], replicated
Inputs may be any that keep to these rules, and one draw needn't show every extreme that they name: Only the first tile_count slots of a block are live; on some block the count is exactly 128. `tile_rows`: A tile position may repeat within a block; repeated tiles add.
All inputs are finite; a program needn't handle non-finite values.
Results may differ from a plain program's by a relative error of at most 0.019.
Values may be sent and summed in bfloat16 or wider, within the bound.
A program may use at most 64 MiB of HBM per device.

v0:
```python
import math
import jax
import jax.numpy as jnp
from jax import lax
from jax.sharding import PartitionSpec as P

BLOCK = 16


def tile_mask(code_block, living):
    tile_side = code_block.shape[1] // 2
    row_code = code_block[:, :tile_side][:, :, None]
    col_code = code_block[:, tile_side:][:, None, :]
    hashed = (row_code * col_code + row_code + 3 * col_code) % 4093
    return ((hashed < 64) & living[:, None, None]).astype(jnp.bfloat16)


def accumulate(codes_dev, rows_dev, cols_dev, count_dev, source, out_tiles, backward):
    tile_side = source.shape[1]
    width_feat = source.shape[2]

    def block_step(block_id, summed):
        slot_start = block_id * BLOCK
        code_block = lax.dynamic_slice_in_dim(codes_dev, slot_start, BLOCK, 0)
        row_block = lax.dynamic_slice_in_dim(rows_dev, slot_start, BLOCK, 0)
        col_block = lax.dynamic_slice_in_dim(cols_dev, slot_start, BLOCK, 0)
        slot_ids = slot_start + jnp.arange(BLOCK, dtype=jnp.int32)
        target = col_block if backward else row_block
        anchor = row_block if backward else col_block
        living = slot_ids < count_dev
        keep = tile_mask(code_block, living)
        picked = jnp.take(source, anchor, axis=0)
        if backward:
            product = jnp.einsum("tij,tif->tjf", keep, picked, preferred_element_type=jnp.float32)
        else:
            product = jnp.einsum("tij,tjf->tif", keep, picked, preferred_element_type=jnp.float32)
        return summed.at[target].add(product)

    start_sum = jnp.zeros((out_tiles, tile_side, width_feat), jnp.float32)
    loop_count = codes_dev.shape[0] // BLOCK
    summed = lax.fori_loop(0, loop_count, block_step, start_sum)
    return summed.reshape(out_tiles * tile_side, width_feat)


def dense_part(aggregate, weight, bias, cotangent, inv_root):
    preact = jnp.dot(aggregate, weight, preferred_element_type=jnp.float32) + bias
    hidden = jax.nn.elu(preact).astype(jnp.bfloat16)
    elu_slope = jnp.where(preact > 0, 1.0, jnp.exp(jnp.minimum(preact, 0.0)))
    grad_pre = cotangent.astype(jnp.float32) * elu_slope
    grad_pre_b = grad_pre.astype(jnp.bfloat16)
    grad_weight = lax.dot_general(
        aggregate, grad_pre_b, (((0,), (0,)), ((), ())), preferred_element_type=jnp.float32
    )
    grad_bias = jnp.sum(grad_pre, axis=0)
    grad_agg = jnp.dot(grad_pre_b, weight.T, preferred_element_type=jnp.float32)
    grad_scaled = (inv_root * grad_agg).astype(jnp.bfloat16)
    return (hidden, grad_weight, grad_bias, grad_scaled)


def local(features, degree, weight, bias, cotangent, tile_rows, tile_cols, tile_count, tile_codes):
    codes_dev = tile_codes[0, 0]
    rows_dev = tile_rows[0, 0]
    cols_dev = tile_cols[0, 0]
    count_dev = tile_count[0, 0, 0]
    pieces = features.shape[0]
    width_feat = features.shape[1]
    tile_side = codes_dev.shape[1] // 2
    row_devs = lax.axis_size("row")
    col_devs = lax.axis_size("col")
    grad_scale = 1.0 / math.sqrt(pieces * row_devs * col_devs)
    row_tiles = pieces * col_devs // tile_side
    col_tiles = pieces * row_devs // tile_side
    inv_root = lax.rsqrt(degree.astype(jnp.float32))[:, None]
    scaled = (inv_root * features.astype(jnp.float32)).astype(jnp.bfloat16)
    column_feats = lax.all_gather(scaled, "row", axis=0, tiled=True).reshape(
        col_tiles, tile_side, width_feat
    )
    row_terms = accumulate(codes_dev, rows_dev, cols_dev, count_dev, column_feats, row_tiles, False)
    agg_sum = lax.psum_scatter(
        row_terms.astype(jnp.bfloat16), "col", scatter_dimension=0, tiled=True
    ).astype(jnp.float32)
    aggregate = (inv_root * agg_sum).astype(jnp.bfloat16)
    hidden, grad_weight, grad_bias, grad_scaled = dense_part(
        aggregate, weight, bias, cotangent, inv_root
    )
    grad_weight, grad_bias = lax.psum(
        (grad_weight * grad_scale, grad_bias * grad_scale), ("row", "col")
    )
    row_grads = lax.all_gather(grad_scaled, "col", axis=0, tiled=True)
    row_sources = row_grads.reshape(row_tiles, tile_side, width_feat)
    col_terms = accumulate(codes_dev, rows_dev, cols_dev, count_dev, row_sources, col_tiles, True)
    grad_sum = lax.psum_scatter(
        col_terms.astype(jnp.bfloat16), "row", scatter_dimension=0, tiled=True
    ).astype(jnp.float32)
    grad_features = (inv_root * grad_sum).astype(jnp.bfloat16)
    return (hidden, grad_features, grad_weight, grad_bias)


def solution(mesh):
    placed = (
        P(("row", "col"), None),
        P(("row", "col")),
        P(),
        P(),
        P(("row", "col"), None),
        P("row", "col", None),
        P("row", "col", None),
        P("row", "col", None),
        P("row", "col", None, None),
    )
    return jax.shard_map(
        local,
        mesh=mesh,
        in_specs=placed,
        out_specs=(P(("row", "col"), None), P(("row", "col"), None), P(), P()),
        check_vma=False,
    )
```

profile of v0, /device:TPU:1, one launch (start us, length us, event | category | flops | bytes accessed | tf_op | source)
XLA Modules:
  0.0 838.8 jit_solution(7499523494927583328)
XLA Ops:
  9.6 86.1 %all-gather.3.cloned.1.call-done = bf16[8192,128]{1,0:T(8,128)(2,1)} async-done(((bf16[256,128]{1,0:T(8,128)(2,1)}), bf16[8192,128]{1,0:T(8,128)(2,1)}) %all-gather.3.cloned.1.call-update) | async-done | bytes 2097168 | tf_op jit(solution)/shard_map/all_gather | solution.py:75
  96.0 66.9 %while.30 = (s32[]{:T(128)}, f32[32,128,128]{2,1,0:T(8,128)S(1)}, s32[128]{0:T(128)S(1)}, s32[128,256]{1,0:T(8,128)}, s32[]{:T(128)}, /*index=5*/s32[128]{0:T(12...) while((s32[]{:T(128)}, f32[32,128,128]{2,1,0:T(8,128)S(1)}, ...), condition=%wide.region_2.3_spmd, body=%wide.region_0.2_spmd.sunk | while | flops 70519992 | bytes 5837511 | solution.py:41
  97.5 3.0 gather_fusion
  105.9 3.0 gather_fusion
  114.2 3.0 gather_fusion
  122.6 3.0 gather_fusion
  131.0 3.0 gather_fusion
  139.3 3.0 gather_fusion
  147.7 3.0 gather_fusion
  156.1 3.0 gather_fusion
  164.1 61.1 %reduce-scatter.3.cloned.1.call-done = bf16[256,128]{1,0:T(8,128)(2,1)} async-done(((bf16[4096,128]{1,0:T(8,128)(2,1)}), bf16[256,128]{1,0:T(8,128)(2,1)}) %reduce-scatter.3.cloned.1.call-update) | async-done | bytes 65552 | tf_op jit(solution)/shard_map/reduce_scatter | solution.py:79
  227.9 43.0 %all-gather.5.cloned.1.call-done = bf16[4096,128]{1,0:T(8,128)(2,1)} async-done(((bf16[256,128]{1,0:T(8,128)(2,1)}), bf16[4096,128]{1,0:T(8,128)(2,1)}) %all-gather.5.cloned.1.call-update) | async-done | bytes 1048592 | tf_op jit(solution)/shard_map/all_gather | solution.py:89
  270.9 2.4 broadcast_in_dim.119
  273.4 63.9 %while.31 = (s32[]{:T(128)}, f32[64,128,128]{2,1,0:T(8,128)}, s32[128]{0:T(128)S(1)}, s32[128,256]{1,0:T(8,128)}, s32[]{:T(128)}, /*index=5*/s32[128]{0:T(128)S(...) while((s32[]{:T(128)}, f32[64,128,128]{2,1,0:T(8,128)}, ...), condition=%wide.region_6.7_spmd, body=%wide.region_4.6_spmd.sunk | while | flops 70519992 | bytes 5837511 | solution.py:41
  275.5 2.4 fusion.63
  278.0 3.4 scatter_fusion.1
  283.5 2.4 fusion.63
  286.0 3.4 scatter_fusion.1
  291.5 2.4 fusion.63
  293.9 3.4 scatter_fusion.1
  299.5 2.4 fusion.63
  301.9 3.4 scatter_fusion.1
  307.5 2.4 fusion.63
  309.9 3.4 scatter_fusion.1
  315.5 2.4 fusion.63
  317.9 3.4 scatter_fusion.1
  325.9 3.4 scatter_fusion.1
  333.9 3.4 scatter_fusion.1
  337.3 3.9 convert_element_type.62
  341.3 98.5 %psum.15 = f32[128]{0:T(128)} all-reduce(f32[128]{0:T(128)S(1)} %broadcast_multiply_fusion.2), channel_id=1, replica_groups=mesh['row'=32,'col'=16] {'row','col'}, use_global_device_ids=true, to_apply=%region_10.11 | all-reduce | flops 128 | bytes 1024 | tf_op jit(solution)/shard_map/psum | solution.py:86
  440.7 117.3 %reduce-scatter.5.cloned.1.call-done = bf16[256,128]{1,0:T(8,128)(2,1)} async-done(((bf16[8192,128]{1,0:T(8,128)(2,1)}), bf16[256,128]{1,0:T(8,128)(2,1)}) %reduce-scatter.5.cloned.1.call-update) | async-done | bytes 65552 | tf_op jit(solution)/shard_map/reduce_scatter | solution.py:92
  559.6 271.2 %all-reduce.2.cloned.1.call-done = f32[128,128]{1,0:T(8,128)} async-done(((f32[128,128]{1,0:T(8,128)}), f32[128,128]{1,0:T(8,128)}) %all-reduce.2.cloned.1.call-update) | async-done | bytes 65552 | tf_op jit(solution)/shard_map/psum | solution.py:86
  (124 shorter events, 75.2 us)
Async XLA Ops:
  7.2 218.1 %copy-start = (bf16[128,128]{1,0:T(8,128)(2,1)S(1)}, bf16[128,128]{1,0:T(8,128)(2,1)}, u32[]{:S(2)}) copy-start(bf16[128,128]{1,0:T(8,128)(2,1)} %param.15) | copy-start | bytes 98308
  7.2 88.8 %copy-start.3 = (s32[1,1,128]{2,1,0:T(1,128)S(1)}, s32[1,1,128]{2,1,0:T(1,128)}, u32[]{:S(2)}) copy-start(s32[1,1,128]{2,1,0:T(1,128)} %param.19) | copy-start | bytes 1540
  7.2 88.8 %copy-start.2 = (s32[1,1,128]{2,1,0:T(1,128)S(1)}, s32[1,1,128]{2,1,0:T(1,128)}, u32[]{:S(2)}) copy-start(s32[1,1,128]{2,1,0:T(1,128)} %param.18) | copy-start | bytes 1540
  7.2 88.5 %all-gather.3.cloned.1.call-start = ((), (), s32[]{:S(2)}) async-start(), calls=%async_computation.2 | async-start | bytes 2162688 | tf_op jit(solution)/shard_map/all_gather | solution.py:75
  9.5 215.7 %reduce-scatter.3.cloned.1.call-start = ((), (), s32[]{:S(2)}) async-start(), calls=%async_computation.3 | async-start | bytes 1114112 | tf_op jit(solution)/shard_map/reduce_scatter | solution.py:79
  162.9 62.3 %copy-start.4 = (bf16[256,128]{1,0:T(8,128)(2,1)S(1)}, bf16[256,128]{1,0:T(8,128)(2,1)}, u32[]{:S(2)}) copy-start(bf16[256,128]{1,0:T(8,128)(2,1)} %param.17) | copy-start | bytes 196612
  162.9 62.3 %copy-start.6 = (f32[128]{0:T(128)S(1)}, f32[128]{0:T(128)}, u32[]{:S(2)}) copy-start(f32[128]{0:T(128)} %param.16) | copy-start | bytes 1540
  164.1 106.8 %all-gather.5.cloned.1.call-start = ((), (), s32[]{:S(2)}) async-start(), calls=%async_computation.4 | async-start | bytes 1114112 | tf_op jit(solution)/shard_map/all_gather | solution.py:89
  227.8 330.2 %reduce-scatter.5.cloned.1.call-start = ((), (), s32[]{:S(2)}) async-start(), calls=%async_computation.5 | async-start | bytes 2162688 | tf_op jit(solution)/shard_map/reduce_scatter | solution.py:92
  270.9 2.5 copy-start.1
  341.2 98.6 %copy-start.5 = (bf16[256,128]{1,0:T(8,128)(2,1)S(1)}, bf16[256,128]{1,0:T(8,128)(2,1)}, u32[]{:S(2)}) copy-start(bf16[256,128]{1,0:T(8,128)(2,1)} %reduce-scatter.3.cloned.1.call-done) | copy-start | bytes 196612
  341.2 489.6 %all-reduce.2.cloned.1.call-start = ((), (), s32[]{:S(2)}) async-start(), calls=%async_computation.6 | async-start | bytes 131072 | tf_op jit(solution)/shard_map/psum | solution.py:86
Sparse Core Ops, SparseCore 0:
  11.8 83.9 all-gather.2
  164.2 60.9 reduce-scatter.2
  227.9 42.9 all-gather.4
  341.3 216.6 reduce-scatter.4
  563.4 267.3 all-reduce.1
where the time goes:
time: 841 us; the launch traced here: 839 us
  waiting for transfers between devices  579 us (69%)
  blocking collectives  98.5 us (12%)
  other arithmetic  73.3 us (9%)
  matrix products  40.1 us (5%)
  local copies, waits for them, and re-layouts  33.5 us (4%)
  between operations  13.9 us (2%)
    psum x1, waiting for transfers between devices, local(): lax.psum((grad_weight * grad_scale, grad_bias * grad_scale), ('row', 'col'))  271 us
    reduce_scatter x1, waiting for transfers between devices, local(): lax.psum_scatter(col_terms.astype(jnp.bfloat16), 'row', scatter_dimension...  117 us
    psum x1, blocking collectives, local(): lax.psum((grad_weight * grad_scale, grad_bias * grad_scale), ('row', 'col'))  98.5 us
    all_gather x1, waiting for transfers between devices, local(): lax.all_gather(scaled, 'row', axis=0, tiled=True)  86.1 us
    reduce_scatter x1, waiting for transfers between devices, local(): lax.psum_scatter(row_terms.astype(jnp.bfloat16), 'col', scatter_dimension...  61.1 us
    all_gather x1, waiting for transfers between devices, local(): row_grads = lax.all_gather(grad_scaled, 'col', axis=0, tiled=True)  43 us
    scatter-add x16, other arithmetic, block_step(): return summed.at[target].add(product)  39.9 us
    gather x16, local copies, waits for them, and re-layouts, block_step(): picked = jnp.take(source, anchor, axis=0)  29.3 us
  transfers between devices with their start and end apart: 5, of which 5 were waited for; matrix products, arithmetic and copies ran while one was open for 0% of the time, Pallas kernels for 0%

commit v1 on v0

--- a/solution.py
+++ b/solution.py
@@ -86,7 +86,9 @@
     grad_weight, grad_bias = lax.psum(
         (grad_weight * grad_scale, grad_bias * grad_scale), ("row", "col")
     )
-    row_grads = lax.all_gather(grad_scaled, "col", axis=0, tiled=True)
+    row_grads = jnp.concatenate(
+        lax.all_to_all(jnp.stack([grad_scaled] * lax.axis_size("col")), "col", 0, 0), axis=0
+    )
     row_sources = row_grads.reshape(row_tiles, tile_side, width_feat)
     col_terms = accumulate(codes_dev, rows_dev, cols_dev, count_dev, row_sources, col_tiles, True)
     grad_sum = lax.psum_scatter(

time: 841 us -> 833 us (level)
  waiting for transfers between devices: 579 us -> 563 us
    all_gather x1 -> x0, waiting for transfers between devices: 43 us -> none  [local(): row_grads = lax.all_gather(grad_scaled, 'col', axis=0, tiled=True)]
    all_to_all x0 -> x1, waiting for transfers between devices: none -> 27.9 us  [local(): lax.all_to_all(jnp.stack([grad_scaled] * lax.axis_size('col')), 'col', 0, 0)]
where the time goes in v1:
time: 833 us; the launch traced here: 831 us
  waiting for transfers between devices  563 us (68%)
  blocking collectives  98.3 us (12%)
  other arithmetic  73.4 us (9%)
  matrix products  39.5 us (5%)
  local copies, waits for them, and re-layouts  34.6 us (4%)
  between operations  13.9 us (2%)
    psum x1, waiting for transfers between devices, local(): lax.psum((grad_weight * grad_scale, grad_bias * grad_scale), ('row', 'col'))  271 us
    reduce_scatter x1, waiting for transfers between devices, local(): lax.psum_scatter(col_terms.astype(jnp.bfloat16), 'row', scatter_dimension...  117 us
    psum x1, blocking collectives, local(): lax.psum((grad_weight * grad_scale, grad_bias * grad_scale), ('row', 'col'))  98.3 us
    all_gather x1, waiting for transfers between devices, local(): lax.all_gather(scaled, 'row', axis=0, tiled=True)  86.1 us
    reduce_scatter x1, waiting for transfers between devices, local(): lax.psum_scatter(row_terms.astype(jnp.bfloat16), 'col', scatter_dimension...  61.1 us
    scatter-add x16, other arithmetic, block_step(): return summed.at[target].add(product)  40 us
    gather x16, local copies, waits for them, and re-layouts, block_step(): picked = jnp.take(source, anchor, axis=0)  29.2 us
    all_to_all x1, waiting for transfers between devices, local(): lax.all_to_all(jnp.stack([grad_scaled] * lax.axis_size('col')), 'col', 0, 0)  27.9 us
  transfers between devices with their start and end apart: 5, of which 5 were waited for; matrix products, arithmetic and copies ran while one was open for 0% of the time, Pallas kernels for 0%

profile of v1, /device:TPU:1, one launch (start us, length us, event | category | flops | bytes accessed | tf_op | source)
XLA Modules:
  0.0 830.6 jit_solution(2668109526447979278)
XLA Ops:
  9.6 86.1 %all-gather.2.cloned.1.call-done = bf16[8192,128]{1,0:T(8,128)(2,1)} async-done(((bf16[256,128]{1,0:T(8,128)(2,1)}), bf16[8192,128]{1,0:T(8,128)(2,1)}) %all-gather.2.cloned.1.call-update) | async-done | bytes 2097168 | tf_op jit(solution)/shard_map/all_gather | solution.py:75
  96.0 66.9 %while.30 = (s32[]{:T(128)}, f32[32,128,128]{2,1,0:T(8,128)S(1)}, s32[128]{0:T(128)S(1)}, s32[128,256]{1,0:T(8,128)}, s32[]{:T(128)}, /*index=5*/s32[128]{0:T(12...) while((s32[]{:T(128)}, f32[32,128,128]{2,1,0:T(8,128)S(1)}, ...), condition=%wide.region_2.3_spmd, body=%wide.region_0.2_spmd.sunk | while | flops 70519992 | bytes 5837511 | solution.py:41
  97.5 3.0 gather_fusion
  105.9 3.0 gather_fusion
  114.2 3.0 gather_fusion
  122.6 3.0 gather_fusion
  130.9 3.0 gather_fusion
  139.3 3.0 gather_fusion
  147.7 3.0 gather_fusion
  156.0 3.0 gather_fusion
  164.0 61.1 %reduce-scatter.3.cloned.1.call-done = bf16[256,128]{1,0:T(8,128)(2,1)} async-done(((bf16[4096,128]{1,0:T(8,128)(2,1)}), bf16[256,128]{1,0:T(8,128)(2,1)}) %reduce-scatter.3.cloned.1.call-update) | async-done | bytes 65552 | tf_op jit(solution)/shard_map/reduce_scatter | solution.py:79
  228.3 7.3 all-to-all-start
  235.6 27.9 %all-to-all-done = bf16[16,256,128]{2,1,0:T(8,128)(2,1)S(1)} async-done(((bf16[16,256,128]{2,1,0:T(8,128)(2,1)}), bf16[16,256,128]{2,1,0:T(8,128)(2,1)S(1)}, u32[]{:S(2)}, u32[]{:S(2)}) %all-to-all-start) | async-done | bytes 1048608 | tf_op jit(solution)/shard_map/all_to_all | solution.py:90
  263.6 2.5 broadcast_in_dim.119
  266.1 64.0 %while.31 = (s32[]{:T(128)}, f32[64,128,128]{2,1,0:T(8,128)}, s32[128]{0:T(128)S(1)}, s32[128,256]{1,0:T(8,128)}, s32[]{:T(128)}, /*index=5*/s32[128]{0:T(128)S(...) while((s32[]{:T(128)}, f32[64,128,128]{2,1,0:T(8,128)}, ...), condition=%wide.region_6.7_spmd, body=%wide.region_4.6_spmd.sunk | while | flops 70519992 | bytes 5837511 | solution.py:41
  270.7 3.4 scatter_fusion.1
  276.3 2.4 fusion.63
  278.7 3.4 scatter_fusion.1
  286.7 3.4 scatter_fusion.1
  292.2 2.4 fusion.63
  294.6 3.4 scatter_fusion.1
  302.7 3.4 scatter_fusion.1
  308.2 2.4 fusion.63
  310.7 3.4 scatter_fusion.1
  316.3 2.4 fusion.63
  318.7 3.4 scatter_fusion.1
  324.3 2.4 fusion.63
  326.7 3.4 scatter_fusion.1
  330.1 3.9 convert_element_type.62
  334.0 98.3 %psum.15 = f32[128]{0:T(128)} all-reduce(f32[128]{0:T(128)S(1)} %broadcast_multiply_fusion.2), channel_id=1, replica_groups=mesh['row'=32,'col'=16] {'row','col'}, use_global_device_ids=true, to_apply=%region_10.11 | all-reduce | flops 128 | bytes 1024 | tf_op jit(solution)/shard_map/psum | solution.py:86
  433.2 116.6 %reduce-scatter.5.cloned.1.call-done = bf16[256,128]{1,0:T(8,128)(2,1)} async-done(((bf16[8192,128]{1,0:T(8,128)(2,1)}), bf16[256,128]{1,0:T(8,128)(2,1)}) %reduce-scatter.5.cloned.1.call-update) | async-done | bytes 65552 | tf_op jit(solution)/shard_map/reduce_scatter | solution.py:94
  551.4 271.2 %all-reduce.2.cloned.1.call-done = f32[128,128]{1,0:T(8,128)} async-done(((f32[128,128]{1,0:T(8,128)}), f32[128,128]{1,0:T(8,128)}) %all-reduce.2.cloned.1.call-update) | async-done | bytes 65552 | tf_op jit(solution)/shard_map/psum | solution.py:86
  (122 shorter events, 78.1 us)
Async XLA Ops:
  7.2 218.0 %copy-start = (bf16[128,128]{1,0:T(8,128)(2,1)S(1)}, bf16[128,128]{1,0:T(8,128)(2,1)}, u32[]{:S(2)}) copy-start(bf16[128,128]{1,0:T(8,128)(2,1)} %param.15) | copy-start | bytes 98308
  7.2 88.8 %copy-start.2 = (s32[1,1,128]{2,1,0:T(1,128)S(1)}, s32[1,1,128]{2,1,0:T(1,128)}, u32[]{:S(2)}) copy-start(s32[1,1,128]{2,1,0:T(1,128)} %param.19) | copy-start | bytes 1540
  7.2 88.8 %copy-start.1 = (s32[1,1,128]{2,1,0:T(1,128)S(1)}, s32[1,1,128]{2,1,0:T(1,128)}, u32[]{:S(2)}) copy-start(s32[1,1,128]{2,1,0:T(1,128)} %param.18) | copy-start | bytes 1540
  7.2 88.5 %all-gather.2.cloned.1.call-start = ((), (), s32[]{:S(2)}) async-start(), calls=%async_computation.3 | async-start | bytes 2162688 | tf_op jit(solution)/shard_map/all_gather | solution.py:75
  9.5 215.6 %reduce-scatter.3.cloned.1.call-start = ((), (), s32[]{:S(2)}) async-start(), calls=%async_computation.4 | async-start | bytes 1114112 | tf_op jit(solution)/shard_map/reduce_scatter | solution.py:79
  162.8 62.3 %copy-start.3 = (bf16[256,128]{1,0:T(8,128)(2,1)S(1)}, bf16[256,128]{1,0:T(8,128)(2,1)}, u32[]{:S(2)}) copy-start(bf16[256,128]{1,0:T(8,128)(2,1)} %param.17) | copy-start | bytes 196612
  162.8 62.3 %copy-start.5 = (f32[128]{0:T(128)S(1)}, f32[128]{0:T(128)}, u32[]{:S(2)}) copy-start(f32[128]{0:T(128)} %param.16) | copy-start | bytes 1540
  228.3 35.3 %all-to-all-start = ((bf16[16,256,128]{2,1,0:T(8,128)(2,1)}), bf16[16,256,128]{2,1,0:T(8,128)(2,1)S(1)}, u32[]{:S(2)}, u32[]{:S(2)}) async-start(bf16[16,256,128]{2,1,0:T(8,128)(2,1)} %stack.2), calls=%async_computation.1 | async-start | bytes 2097152 | tf_op jit(solution)/shard_map/all_to_all | solution.py:90
  235.6 314.3 %reduce-scatter.5.cloned.1.call-start = ((), (), s32[]{:S(2)}) async-start(), calls=%async_computation.5 | async-start | bytes 2162688 | tf_op jit(solution)/shard_map/reduce_scatter | solution.py:94
  334.0 98.4 %copy-start.4 = (bf16[256,128]{1,0:T(8,128)(2,1)S(1)}, bf16[256,128]{1,0:T(8,128)(2,1)}, u32[]{:S(2)}) copy-start(bf16[256,128]{1,0:T(8,128)(2,1)} %reduce-scatter.3.cloned.1.call-done) | copy-start | bytes 196612
  334.0 488.6 %all-reduce.2.cloned.1.call-start = ((), (), s32[]{:S(2)}) async-start(), calls=%async_computation.6 | async-start | bytes 131072 | tf_op jit(solution)/shard_map/psum | solution.py:86
Sparse Core Ops, SparseCore 0:
  11.8 83.9 all-gather.1
  164.1 60.9 reduce-scatter.2
  334.1 215.7 reduce-scatter.4
  555.3 267.2 all-reduce.1
